TPU v7x, 256 devices: a whole 4x4x8 slice. The times are simulated.
256 devices in a mesh: ctx: 8 (over z), chan: 32 (over x, y, core).
Axes of the slice: x: 4, y: 4, z: 8, core: 2. Of those that a mesh axis runs over, the one named last changes fastest.
Arguments:
- query_rows: bfloat16 [2048, 8192], P('ctx', 'chan'), may hold values from -6 to 6
- key_rows: bfloat16 [2048, 8192], P('ctx', 'chan'), may hold values from -6 to 6
- value_rows: bfloat16 [2048, 8192], P('ctx', 'chan'), may hold values from -6 to 6
- short_taps: float32 [3, 3, 8192], P(None, None, 'chan'), may hold values from -3 to 3
- long_filter: bfloat16 [2048, 8192], P('ctx', 'chan'), may hold values from -4 to 4
- direction: bfloat16 [2048, 8192], P('ctx', 'chan'), may hold values from -4 to 4
- w_out: bfloat16 [8192, 8192], P('chan'), may hold values from -0.125 to 0.125
- target: bfloat16 [2048, 8192], P('ctx'), may hold values from -6 to 6
Outputs:
- grad_filter: float32 [2048, 8192], P('ctx', 'chan')
- hvp_filter: float32 [2048, 8192], P('ctx', 'chan')
All inputs are finite; a program needn't handle non-finite values.
Results may differ from a plain program's by a relative error of at most 0.033.
Values may be sent and summed in bfloat16 or wider, within the bound.
A program may use at most 128 MiB of HBM per device.

v0:
```python
import math
import jax
import jax.numpy as jnp
from jax import lax
from jax.sharding import PartitionSpec as P


def passed_along(value, axis, steps):
    count = lax.axis_size(axis)
    initial, last = (max(0, -steps), min(count, count - steps))
    return lax.ppermute(value, axis, [(source, source + steps) for source in range(initial, last)])


def short_conv(current, earlier, coeffs):
    extended = jnp.concatenate([earlier.astype(jnp.float32), current.astype(jnp.float32)], axis=0)
    length = current.shape[0]
    return (
        coeffs[0] * extended[2 : 2 + length]
        + coeffs[1] * extended[1 : 1 + length]
        + coeffs[2] * extended[0:length]
    )


def depthwise(window, kernel):
    result = lax.conv_general_dilated(
        window[None],
        kernel[:, None, :],
        (1,),
        "VALID",
        dimension_numbers=("NHC", "HIO", "NHC"),
        feature_group_count=window.shape[1],
        preferred_element_type=jnp.float32,
    )
    return result[0]


def paired(window, first_kernel, second_kernel):
    return jax.vmap(lambda kernel: depthwise(window, kernel))(
        jnp.stack([first_kernel, second_kernel])
    )


def on_device(query_rows, key_rows, value_rows, short_taps, long_filter, direction, w_out, target):
    block_len = query_rows.shape[0]
    chan_width = query_rows.shape[1]
    earlier = passed_along(
        (query_rows[block_len - 2 :], key_rows[block_len - 2 :], value_rows[block_len - 2 :]),
        "ctx",
        1,
    )
    taps_all, dir_all = (
        lax.all_gather(long_filter, "ctx", axis=0, tiled=True),
        lax.all_gather(direction, "ctx", axis=0, tiled=True),
    )
    gate_in = short_conv(query_rows, earlier[0], short_taps[0])
    key_short = short_conv(key_rows, earlier[1], short_taps[1])
    value_short = short_conv(value_rows, earlier[2], short_taps[2])
    mixed_rows = (key_short * value_short).astype(jnp.bfloat16)
    history = lax.all_gather(mixed_rows, "ctx", axis=0, tiled=True)
    seq_total = history.shape[0]
    my_block = lax.axis_index("ctx")
    padded = jnp.concatenate([jnp.zeros((block_len, chan_width), jnp.bfloat16), history], axis=0)

    def window_at(distance):
        return lax.dynamic_slice_in_dim(padded, distance * block_len + 1, 2 * block_len - 1, 0)

    def forward_step(tap_block, running):
        window = window_at(my_block - tap_block)
        taps_here = lax.dynamic_slice_in_dim(taps_all, tap_block * block_len, block_len, 0)[::-1]
        dirs_here = lax.dynamic_slice_in_dim(dir_all, tap_block * block_len, block_len, 0)[::-1]
        return running + paired(window, taps_here, dirs_here)

    convolved = lax.fori_loop(
        0, my_block + 1, forward_step, jnp.zeros((2, block_len, chan_width), jnp.float32)
    )
    gated_rows = (gate_in * convolved[0]).astype(jnp.bfloat16)
    gated_dir = (gate_in * convolved[1]).astype(jnp.bfloat16)
    stacked = jnp.concatenate([gated_rows, gated_dir], axis=0)
    scaling = 1.0 / math.sqrt(seq_total)
    summed = lax.psum_scatter(
        lax.dot_general(
            w_out, stacked, (((0,), (1,)), ((), ())), preferred_element_type=jnp.float32
        ).astype(jnp.bfloat16),
        "chan",
        scatter_dimension=0,
        tiled=True,
    ).astype(jnp.float32)
    column_start = lax.axis_index("chan") * chan_width
    target_mine = (
        lax.dynamic_slice_in_dim(target, column_start, chan_width, 1).astype(jnp.float32).T
    )
    bent_out = jnp.tanh(summed[:, :block_len] - target_mine)
    cot_grad = (scaling * bent_out).astype(jnp.bfloat16)
    cot_hvp = (scaling * (1.0 - bent_out * bent_out) * summed[:, block_len:]).astype(jnp.bfloat16)
    cotangent = jnp.concatenate([cot_grad, cot_hvp], axis=1)
    backward = jnp.dot(
        w_out,
        lax.all_gather(cotangent, "chan", axis=0, tiled=True),
        preferred_element_type=jnp.float32,
    )
    back_grad = backward[:, :block_len].T
    back_hvp = backward[:, block_len:].T
    dz_grad = (gate_in * back_grad).astype(jnp.bfloat16)
    dz_hvp = (gate_in * back_hvp).astype(jnp.bfloat16)

    def backward_step(tap_block, running):
        window = window_at(my_block - tap_block)
        pair = paired(window, dz_grad, dz_hvp)[:, ::-1]
        placed = jnp.concatenate([pair[0], pair[1]], axis=1)
        return lax.dynamic_update_slice_in_dim(running, placed, tap_block * block_len, 0)

    tap_terms = lax.fori_loop(
        0, my_block + 1, backward_step, jnp.zeros((seq_total, 2 * chan_width), jnp.float32)
    )
    shares = lax.psum_scatter(
        tap_terms.astype(jnp.bfloat16), "ctx", scatter_dimension=0, tiled=True
    ).astype(jnp.float32)
    return (shares[:, :chan_width], shares[:, chan_width:])


def solution(mesh):
    in_specs = (
        P("ctx", "chan"),
        P("ctx", "chan"),
        P("ctx", "chan"),
        P(None, None, "chan"),
        P("ctx", "chan"),
        P("ctx", "chan"),
        P("chan", None),
        P("ctx", None),
    )
    out_specs = (P("ctx", "chan"), P("ctx", "chan"))
    return jax.shard_map(
        on_device, mesh=mesh, in_specs=in_specs, out_specs=out_specs, check_vma=False
    )
```

profile of v0, /device:TPU:2, one launch (start us, length us, event | category | flops | bytes accessed | tf_op | source)
XLA Modules:
  0.0 615.9 jit_solution(8180843435490185184)
XLA Ops:
  7.2 0.0 all-gather.5.cloned.1.call-start
  7.2 0.7 slice.125
  7.9 3.8 collective-permute-start
  11.7 0.7 slice.131
  12.4 3.8 collective-permute-start.1
  16.2 1.5 fusion.41
  17.7 0.9 convert_element_type.55
  18.6 0.9 convert_element_type.57
  19.5 0.0 collective-permute-done
  19.6 0.0 collective-permute-done.1
  19.6 0.8 fusion.14
  20.4 0.0 all-gather.5.cloned.1.call-update
  20.4 0.0 all-gather.7.cloned.1.call-start
  20.5 0.7 all-gather.7.cloned.1.call-update
  21.2 0.0 all-gather.9.cloned.1.call-start
  21.2 0.7 all-gather.9.cloned.1.call-update
  21.9 0.0 reduce-scatter.3.cloned.1.call-start
  22.0 0.7 slice.137
  22.7 3.8 collective-permute-start.2
  26.5 1.6 convert_element_type.60
  28.1 0.0 collective-permute-done.2
  28.1 0.6 convert_element_type.61
  28.7 31.8 %all-gather.5.cloned.1.call-done = bf16[2048,256]{1,0:T(8,128)(2,1)} async-done(((bf16[256,256]{1,0:T(8,128)(2,1)}), bf16[2048,256]{1,0:T(8,128)(2,1)}) %all-gather.5.cloned.1.call-update) | async-done | bytes 1048592 | tf_op jit(solution)/shard_map/all_gather | solution.py:59
  60.6 1.3 concatenate.26
  61.9 37.3 %all-gather.7.cloned.1.call-done = bf16[2048,256]{1,0:T(8,128)(2,1)} async-done(((bf16[256,256]{1,0:T(8,128)(2,1)}), bf16[2048,256]{1,0:T(8,128)(2,1)}) %all-gather.7.cloned.1.call-update) | async-done | bytes 1048592 | tf_op jit(solution)/shard_map/all_gather | solution.py:52
  99.2 38.6 %all-gather.9.cloned.1.call-done = bf16[2048,256]{1,0:T(8,128)(2,1)} async-done(((bf16[256,256]{1,0:T(8,128)(2,1)}), bf16[2048,256]{1,0:T(8,128)(2,1)}) %all-gather.9.cloned.1.call-update) | async-done | bytes 1048592 | tf_op jit(solution)/shard_map/all_gather | solution.py:53
  137.8 0.1 broadcast_in_dim.22
  138.0 0.0 copy-start
  138.0 15.6 %while.24 = (s32[]{:T(128)}, f32[2,256,256]{2,0,1:T(2,128)S(1)}, s32[]{:T(128)}, s32[]{:T(128)}, bf16[2304,256]{1,0:T(8,128)(2,1)S(1)}, /*index=5*/bf16[2048,256...) while((s32[]{:T(128)}, f32[2,256,256]{2,0,1:T(2,128)S(1)}, ...), condition=%wide.region_1.0_spmd, body=%wide.region_0.0_spmd.sunk | while | flops 67371016 | bytes 4717297 | solution.py:73
  138.0 1.0 constant_dynamic-slice_fusion.3
  139.1 0.2 rev.15
  139.3 0.2 rev.16
  139.5 0.1 dynamic-slice_bitcast_fusion.4
  139.6 13.5 %convolution_bitcast_fusion.5 = f32[2,1,256,256]{3,1,0,2:T(1,128)S(1)} fusion(bf16[256,1,256,2]{2,0,3,1:T(8,128)(2,1)S(1)} %maximum_bitcast_fusion.2, bf16[1,511,256,1]{2,1,3,0:T(8,128)(2,1)S(1)} %dynamic-slice_bitcast_fusion.4), kind=kOutput, calls=%fused_computation.clone.1 | convolution fusion | flops 67108864 | bytes 1048064 | tf_op jit(solution)/shard_map/convolution.6
  153.1 0.6 bitcast_add_fusion.2
  153.7 0.0 copy-done
  153.7 0.0 copy-done.1
  153.7 0.0 copy-done.2
  153.7 0.0 copy-done.3
  153.7 0.1 fusion.28
  153.9 7.8 %fusion.4 = bf16[8192,512]{0,1:T(8,128)(2,1)} fusion(bf16[256,8192]{1,0:T(8,128)(2,1)} %param.18, bf16[256,256]{1,0:T(8,128)(2,1)S(1)} %fusion.26, bf16[256,256]{1,0:T(8,128)(2,1)S(1)} %get-tuple-element.225), kind=kOutput, calls=%fused_computation.17 | convolution fusion | flops 2152202240 | bytes 12845056 | tf_op jit(solution)/shard_map/dot_general | solution.py:81
  161.7 0.0 reduce-scatter.3.cloned.1.call-update
  161.7 0.0 all-gather.11.cloned.1.call-start
  161.8 206.3 %reduce-scatter.3.cloned.1.call-done = bf16[256,512]{0,1:T(8,128)(2,1)} async-done(((bf16[8192,512]{0,1:T(8,128)(2,1)}), bf16[256,512]{0,1:T(8,128)(2,1)}) %reduce-scatter.3.cloned.1.call-update) | async-done | bytes 262160 | tf_op jit(solution)/shard_map/reduce_scatter | solution.py:80
  368.0 1.0 convert_element_type.66
  369.0 1.0 multiply_convert_fusion
  370.0 0.7 pad_maximum_fusion.3
  370.7 0.0 all-gather.11.cloned.1.call-update
  370.8 0.2 reduce-scatter.5.cloned.1.call-start
  371.0 63.1 %all-gather.11.cloned.1.call-done = bf16[8192,512]{0,1:T(8,128)(2,1)} async-done(((bf16[256,512]{0,1:T(8,128)(2,1)}), bf16[8192,512]{0,1:T(8,128)(2,1)}) %all-gather.11.cloned.1.call-update) | async-done | bytes 8388624 | tf_op jit(solution)/shard_map/all_gather | solution.py:98
  434.1 6.9 %convolution_bitcast_fusion.2 = f32[256,512]{0,1:T(8,128)S(1)} fusion(bf16[8192,512]{0,1:T(8,128)(2,1)} %all-gather.11.cloned.1.call-done, bf16[256,8192]{1,0:T(8,128)(2,1)} %param.18), kind=kOutput, calls=%fused_computation.18 | convolution fusion | flops 2147483648 | bytes 13107200 | tf_op jit(solution)/shard_map/dot_general | solution.py:96
  441.0 0.1 fusion.35
  441.1 0.3 copy.22
  441.4 1.5 broadcast_in_dim.21
  442.9 15.5 %while.25 = (s32[]{:T(128)}, bf16[2048,512]{1,0:T(8,128)(2,1)}, s32[]{:T(128)}, s32[]{:T(128)}, bf16[2304,256]{1,0:T(8,128)(2,1)S(1)}, /*index=5*/bf16[2,256,256...) while((s32[]{:T(128)}, bf16[2048,512]{1,0:T(8,128)(2,1)}, ...), condition=%wide.region_4.0_spmd, body=%wide.region_3.0_spmd.sunk | while | flops 67633160 | bytes 3406569 | solution.py:112
  442.9 0.1 dynamic-slice_bitcast_fusion.5
  442.9 13.6 %convolution_bitcast_fusion.6 = bf16[2,1,256,256]{3,1,0,2:T(2,128)(2,1)S(1)} fusion(bf16[256,1,256,2]{2,3,0,1:T(2,128)(2,1)S(1)} %bitcast.127, bf16[1,511,256,1]{2,1,3,0:T(8,128)(2,1)S(1)} %dynamic-slice_bitcast_fusion.5), kind=kOutput, calls=%fused_computation.8.clone.1 | convolution fusion | flops 67108864 | bytes 785920 | tf_op jit(solution)/shard_map/convolution.7
  456.5 0.5 fusion.54
  457.1 0.3 slice.260
  457.4 0.2 slice.261
  457.6 0.7 maximum_dynamic-update-slice_fusion.2
  458.3 0.0 reduce-scatter.5.cloned.1.call-update
  458.4 148.9 %reduce-scatter.5.cloned.1.call-done = bf16[256,512]{1,0:T(8,128)(2,1)} async-done(((bf16[2048,512]{1,0:T(8,128)(2,1)}), bf16[256,512]{1,0:T(8,128)(2,1)}) %reduce-scatter.5.cloned.1.call-update) | async-done | bytes 262160 | tf_op jit(solution)/shard_map/reduce_scatter | solution.py:115
  607.2 1.8 fusion.40
  (13 shorter events, 0.2 us)
Async XLA Ops:
  7.2 53.4 %all-gather.5.cloned.1.call-start = ((), (), s32[]{:S(2)}) async-start(), calls=%async_computation.2 | async-start | bytes 1179648 | tf_op jit(solution)/shard_map/all_gather | solution.py:59
  7.9 11.6 %collective-permute-start = (bf16[2,256]{1,0:T(2,128)(2,1)S(1)}, bf16[2,256]{1,0:T(2,128)(2,1)S(1)}, u32[]{:S(2)}, u32[]{:S(2)}) collective-permute-start(bf16[2,256]{1,0:T(2,128)(2,1)S(1)} %slice.125), channel_id=1, source_target_pairs={{0,32},{32,64},{64,96},{96,128},{128,160},{160,192},{192,224},{1,3... | collective-permute-start | bytes 3080 | tf_op jit(solution)/shard_map/ppermute | solution.py:11
  12.4 7.2 %collective-permute-start.1 = (bf16[2,256]{1,0:T(2,128)(2,1)S(1)}, bf16[2,256]{1,0:T(2,128)(2,1)S(1)}, u32[]{:S(2)}, u32[]{:S(2)}) collective-permute-start(bf16[2,256]{1,0:T(2,128)(2,1)S(1)} %slice.131), channel_id=1, source_target_pairs={{0,32},{32,64},{64,96},{96,128},{128,160},{160,192},{192,224},{1,3... | collective-permute-start | bytes 3080 | tf_op jit(solution)/shard_map/ppermute | solution.py:11
  20.4 78.7 %all-gather.7.cloned.1.call-start = ((), (), s32[]{:S(2)}) async-start(), calls=%async_computation.3 | async-start | bytes 1179648 | tf_op jit(solution)/shard_map/all_gather | solution.py:52
  21.2 116.6 %all-gather.9.cloned.1.call-start = ((), (), s32[]{:S(2)}) async-start(), calls=%async_computation.4 | async-start | bytes 1179648 | tf_op jit(solution)/shard_map/all_gather | solution.py:53
  21.9 346.1 %reduce-scatter.3.cloned.1.call-start = ((), (), s32[]{:S(2)}) async-start(), calls=%async_computation.5 | async-start | bytes 8650752 | tf_op jit(solution)/shard_map/reduce_scatter | solution.py:80
  22.7 5.5 collective-permute-start.2
  138.0 15.7 %copy-start = (f32[256,256]{1,0:T(8,128)S(1)}, f32[256,256]{1,0:T(8,128)}, u32[]{:S(2)}) copy-start(f32[256,256]{1,0:T(8,128)} %convert_element_type.60) | copy-start | bytes 786436
  138.0 15.7 %copy-start.1 = (f32[2,256]{1,0:T(2,128)S(1)}, f32[2,256]{1,0:T(2,128)}, u32[]{:S(2)}) copy-start(f32[2,256]{1,0:T(2,128)} %convert_element_type.61) | copy-start | bytes 6148
  138.0 15.7 %copy-start.2 = (f32[1,1,256]{2,1,0:T(1,128)S(1)}, f32[1,1,256]{2,1,0:T(1,128)}, u32[]{:S(2)}) copy-start(f32[1,1,256]{2,1,0:T(1,128)} %get-tuple-element.237) | copy-start | bytes 3076
  138.0 15.7 %copy-start.3 = (f32[1,1,256]{2,1,0:T(1,128)S(1)}, f32[1,1,256]{2,1,0:T(1,128)}, u32[]{:S(2)}) copy-start(f32[1,1,256]{2,1,0:T(1,128)} %get-tuple-element.244) | copy-start | bytes 3076
  138.0 15.7 %copy-start.4 = (f32[1,1,256]{2,1,0:T(1,128)S(1)}, f32[1,1,256]{2,1,0:T(1,128)}, u32[]{:S(2)}) copy-start(f32[1,1,256]{2,1,0:T(1,128)} %get-tuple-element.245) | copy-start | bytes 3076
  161.7 272.4 %all-gather.11.cloned.1.call-start = ((), (), s32[]{:S(2)}) async-start(), calls=%async_computation.6 | async-start | bytes 8650752 | tf_op jit(solution)/shard_map/all_gather | solution.py:98
  370.8 236.5 %reduce-scatter.5.cloned.1.call-start = ((), (), s32[]{:S(2)}) async-start(), calls=%async_computation.7 | async-start | bytes 2359296 | tf_op jit(solution)/shard_map/reduce_scatter | solution.py:115
Sparse Core Ops, SparseCore 0:
  20.6 39.9 all-gather.4
  62.4 36.7 all-gather.6
  101.0 36.7 all-gather.8
  161.8 206.1 reduce-scatter.2
  370.9 63.1 all-gather.10
  458.5 148.7 reduce-scatter.4
where the time goes:
time: 616 us
  waiting for transfers between devices  527 us (86%)
  matrix products  41.8 us (7%)
  between operations  14.3 us (2%)
  starting transfers between devices  11.9 us (2%)
  local copies, waits for them, and re-layouts  11.1 us (2%)
  other arithmetic  9.17 us (1%)
    reduce_scatter x1, waiting for transfers between devices, on_device(): lax.psum_scatter(lax.dot_general(w_out, stacked, (((0,), (1,)), ((), ()))...  206 us
    reduce_scatter x1, waiting for transfers between devices, on_device(): lax.psum_scatter(tap_terms.astype(jnp.bfloat16), 'ctx', scatter_dimension...  149 us
    all_gather x1, waiting for transfers between devices, on_device(): lax.all_gather(cotangent, 'chan', axis=0, tiled=True)  63.1 us
    all_gather x1, waiting for transfers between devices, on_device(): lax.all_gather(direction, 'ctx', axis=0, tiled=True)  38.6 us
    all_gather x1, waiting for transfers between devices, on_device(): lax.all_gather(long_filter, 'ctx', axis=0, tiled=True)  37.3 us
    all_gather x1, waiting for transfers between devices, on_device(): history = lax.all_gather(mixed_rows, 'ctx', axis=0, tiled=True)  31.8 us
    another operation x2, matrix products  27.1 us
  transfers between devices with their start and end apart: 9, of which 6 were waited for; matrix products, arithmetic and copies ran while one was open for 1% of the time, Pallas kernels for 0%

commit v1 on v0

--- a/solution.py
+++ b/solution.py
@@ -56,7 +56,9 @@
     key_short = short_conv(key_rows, earlier[1], short_taps[1])
     value_short = short_conv(value_rows, earlier[2], short_taps[2])
     mixed_rows = (key_short * value_short).astype(jnp.bfloat16)
-    history = lax.all_gather(mixed_rows, "ctx", axis=0, tiled=True)
+    history = jnp.concatenate(
+        lax.all_to_all(jnp.stack([mixed_rows] * lax.axis_size("ctx")), "ctx", 0, 0), axis=0
+    )
     seq_total = history.shape[0]
     my_block = lax.axis_index("ctx")
     padded = jnp.concatenate([jnp.zeros((block_len, chan_width), jnp.bfloat16), history], axis=0)

time: 616 us -> 580 us (0.942)
  waiting for transfers between devices: 527 us -> 486 us
  starting transfers between devices: 11.9 us -> 19 us
    all_gather x1, waiting for transfers between devices: 37.3 us -> 0.02 us  [on_device(): lax.all_gather(long_filter, 'ctx', axis=0, tiled=True)]
    all_gather x1 -> x0, waiting for transfers between devices: 31.8 us -> none  [on_device(): history = lax.all_gather(mixed_rows, 'ctx', axis=0, tiled=True)]
    ppermute x3, waiting for transfers between devices: 0.01 us -> 22.2 us  [passed_along(): lax.ppermute(value, axis, [(source, source + steps) for source in range(i...]
    all_to_all x0 -> x1, starting transfers between devices: none -> 7.07 us  [on_device(): lax.all_to_all(jnp.stack([mixed_rows] * lax.axis_size('ctx')), 'ctx', 0, 0)]
where the time goes in v1:
time: 580 us; the launch traced here: 579 us
  waiting for transfers between devices  486 us (84%)
  matrix products  41.8 us (7%)
  starting transfers between devices  19 us (3%)
  between operations  14 us (2%)
  local copies, waits for them, and re-layouts  10.3 us (2%)
  other arithmetic  7.59 us (1%)
    reduce_scatter x1, waiting for transfers between devices, on_device(): lax.psum_scatter(lax.dot_general(w_out, stacked, (((0,), (1,)), ((), ()))...  206 us
    reduce_scatter x1, waiting for transfers between devices, on_device(): lax.psum_scatter(tap_terms.astype(jnp.bfloat16), 'ctx', scatter_dimension...  149 us
    all_gather x1, waiting for transfers between devices, on_device(): lax.all_gather(cotangent, 'chan', axis=0, tiled=True)  63.1 us
    all_gather x1, waiting for transfers between devices, on_device(): lax.all_gather(direction, 'ctx', axis=0, tiled=True)  39.4 us
    another operation x2, matrix products  27.1 us
    ppermute x3, waiting for transfers between devices, passed_along(): lax.ppermute(value, axis, [(source, source + steps) for source in range(i...  22.2 us
  transfers between devices with their start and end apart: 9, of which 6 were waited for; matrix products, arithmetic and copies ran while one was open for 1% of the time, Pallas kernels for 0%

profile of v1, /device:TPU:2, one launch (start us, length us, event | category | flops | bytes accessed | tf_op | source)
XLA Modules:
  0.0 579.1 jit_solution(885201320377437420)
XLA Ops:
  7.2 0.0 copy-start.1
  7.2 0.0 all-gather.4.cloned.1.call-start
  7.2 0.7 all-gather.4.cloned.1.call-update
  7.9 0.7 slice.125
  8.6 3.8 collective-permute-start
  12.4 0.7 slice.131
  13.1 3.8 collective-permute-start.1
  16.9 1.4 fusion.41
  18.4 0.9 convert_element_type.55
  19.3 0.9 convert_element_type.57
  20.2 0.0 collective-permute-done
  20.3 0.0 collective-permute-done.1
  20.3 0.2 fusion.14
  20.5 1.1 stack.44
  21.5 7.1 %all-to-all-start = ((bf16[8,256,256]{2,1,0:T(8,128)(2,1)}), bf16[8,256,256]{2,1,0:T(8,128)(2,1)S(1)}, u32[]{:S(2)}, u32[]{:S(2)}) async-start(bf16[8,256,256]{2,1,0:T(8,128)(2,1)} %stack.44), calls=%async_computation | async-start | bytes 2097152 | tf_op jit(solution)/shard_map/all_to_all | solution.py:60
  28.6 0.0 all-gather.6.cloned.1.call-start
  28.6 0.7 all-gather.6.cloned.1.call-update
  29.3 0.0 reduce-scatter.3.cloned.1.call-start
  29.4 0.0 copy-done.1
  29.4 3.9 collective-permute-start.2
  33.3 0.7 convert_element_type.60
  34.0 22.2 %collective-permute-done.2 = bf16[2,256]{1,0:T(2,128)(2,1)S(1)} collective-permute-done((bf16[2,256]{1,0:T(2,128)(2,1)S(1)}, bf16[2,256]{1,0:T(2,128)(2,1)S(1)}, u32[]{:S(2)}, u32[]{:S(2)}) %collective-permute-start.2) | collective-permute-done | bytes 1056 | tf_op jit(solution)/shard_map/ppermute | solution.py:11
  56.2 0.6 convert_element_type.61
  56.8 5.0 all-to-all-done
  61.8 0.1 concatenate.26
  61.9 0.0 all-gather.4.cloned.1.call-done
  61.9 39.4 %all-gather.6.cloned.1.call-done = bf16[2048,256]{1,0:T(8,128)(2,1)} async-done(((bf16[256,256]{1,0:T(8,128)(2,1)}), bf16[2048,256]{1,0:T(8,128)(2,1)}) %all-gather.6.cloned.1.call-update) | async-done | bytes 1048592 | tf_op jit(solution)/shard_map/all_gather | solution.py:53
  101.3 0.1 broadcast_in_dim.22
  101.5 0.0 copy-start
  101.5 0.0 copy-start.2
  101.5 0.0 copy-start.3
  101.5 0.0 copy-start.4
  101.5 15.6 %while.24 = (s32[]{:T(128)}, f32[2,256,256]{2,0,1:T(2,128)S(1)}, s32[]{:T(128)}, s32[]{:T(128)}, bf16[2304,256]{1,0:T(8,128)(2,1)S(1)}, /*index=5*/bf16[2048,256...) while((s32[]{:T(128)}, f32[2,256,256]{2,0,1:T(2,128)S(1)}, ...), condition=%wide.region_1.0_spmd, body=%wide.region_0.0_spmd.sunk | while | flops 67371016 | bytes 4717297 | solution.py:75
  101.5 1.0 constant_dynamic-slice_fusion.3
  102.5 0.2 rev.15
  102.7 0.2 rev.16
  103.0 0.1 dynamic-slice_bitcast_fusion.4
  103.1 13.5 %convolution_bitcast_fusion.5 = f32[2,1,256,256]{3,1,0,2:T(1,128)S(1)} fusion(bf16[256,1,256,2]{2,0,3,1:T(8,128)(2,1)S(1)} %maximum_bitcast_fusion.2, bf16[1,511,256,1]{2,1,3,0:T(8,128)(2,1)S(1)} %dynamic-slice_bitcast_fusion.4), kind=kOutput, calls=%fused_computation.clone.1 | convolution fusion | flops 67108864 | bytes 1048064 | tf_op jit(solution)/shard_map/convolution.6
  116.5 0.6 bitcast_add_fusion.2
  117.2 0.1 fusion.28
  117.4 7.8 %fusion.4 = bf16[8192,512]{0,1:T(8,128)(2,1)} fusion(bf16[256,8192]{1,0:T(8,128)(2,1)} %param.18, bf16[256,256]{1,0:T(8,128)(2,1)S(1)} %fusion.26, bf16[256,256]{1,0:T(8,128)(2,1)S(1)} %get-tuple-element.225), kind=kOutput, calls=%fused_computation.17 | convolution fusion | flops 2152202240 | bytes 12845056 | tf_op jit(solution)/shard_map/dot_general | solution.py:83
  125.2 0.0 reduce-scatter.3.cloned.1.call-update
  125.2 0.0 all-gather.8.cloned.1.call-start
  125.3 206.3 %reduce-scatter.3.cloned.1.call-done = bf16[256,512]{0,1:T(8,128)(2,1)} async-done(((bf16[8192,512]{0,1:T(8,128)(2,1)}), bf16[256,512]{0,1:T(8,128)(2,1)}) %reduce-scatter.3.cloned.1.call-update) | async-done | bytes 262160 | tf_op jit(solution)/shard_map/reduce_scatter | solution.py:82
  331.5 1.0 convert_element_type.66
  332.5 1.0 multiply_convert_fusion
  333.5 0.7 pad_maximum_fusion.3
  334.2 0.0 all-gather.8.cloned.1.call-update
  334.3 0.2 reduce-scatter.5.cloned.1.call-start
  334.5 63.1 %all-gather.8.cloned.1.call-done = bf16[8192,512]{0,1:T(8,128)(2,1)} async-done(((bf16[256,512]{0,1:T(8,128)(2,1)}), bf16[8192,512]{0,1:T(8,128)(2,1)}) %all-gather.8.cloned.1.call-update) | async-done | bytes 8388624 | tf_op jit(solution)/shard_map/all_gather | solution.py:100
  397.6 6.9 %convolution_bitcast_fusion.2 = f32[256,512]{0,1:T(8,128)S(1)} fusion(bf16[8192,512]{0,1:T(8,128)(2,1)} %all-gather.8.cloned.1.call-done, bf16[256,8192]{1,0:T(8,128)(2,1)} %param.18), kind=kOutput, calls=%fused_computation.18 | convolution fusion | flops 2147483648 | bytes 13107200 | tf_op jit(solution)/shard_map/dot_general | solution.py:98
  404.5 0.1 fusion.35
  404.6 0.3 copy.22
  404.9 1.5 broadcast_in_dim.21
  406.4 15.5 %while.25 = (s32[]{:T(128)}, bf16[2048,512]{1,0:T(8,128)(2,1)}, s32[]{:T(128)}, s32[]{:T(128)}, bf16[2304,256]{1,0:T(8,128)(2,1)S(1)}, /*index=5*/bf16[2,256,256...) while((s32[]{:T(128)}, bf16[2048,512]{1,0:T(8,128)(2,1)}, ...), condition=%wide.region_4.0_spmd, body=%wide.region_3.0_spmd.sunk | while | flops 67633160 | bytes 3406569 | solution.py:114
  406.4 0.1 dynamic-slice_bitcast_fusion.5
  406.4 13.6 %convolution_bitcast_fusion.6 = bf16[2,1,256,256]{3,1,0,2:T(2,128)(2,1)S(1)} fusion(bf16[256,1,256,2]{2,3,0,1:T(2,128)(2,1)S(1)} %bitcast.129, bf16[1,511,256,1]{2,1,3,0:T(8,128)(2,1)S(1)} %dynamic-slice_bitcast_fusion.5), kind=kOutput, calls=%fused_computation.8.clone.1 | convolution fusion | flops 67108864 | bytes 785920 | tf_op jit(solution)/shard_map/convolution.7
  420.0 0.5 fusion.54
  420.6 0.3 slice.260
  420.9 0.2 slice.261
  421.1 0.7 maximum_dynamic-update-slice_fusion.2
  421.8 0.0 reduce-scatter.5.cloned.1.call-update
  421.9 148.9 %reduce-scatter.5.cloned.1.call-done = bf16[256,512]{1,0:T(8,128)(2,1)} async-done(((bf16[2048,512]{1,0:T(8,128)(2,1)}), bf16[256,512]{1,0:T(8,128)(2,1)}) %reduce-scatter.5.cloned.1.call-update) | async-done | bytes 262160 | tf_op jit(solution)/shard_map/reduce_scatter | solution.py:117
  570.7 1.8 fusion.40
  (15 shorter events, 0.2 us)
Async XLA Ops:
  7.2 22.2 %copy-start.1 = (bf16[256,256]{1,0:T(8,128)(2,1)S(1)}, bf16[256,256]{1,0:T(8,128)(2,1)}, u32[]{:S(2)}) copy-start(bf16[256,256]{1,0:T(8,128)(2,1)} %param.12) | copy-start | bytes 393220
  7.2 54.7 %all-gather.4.cloned.1.call-start = ((), (), s32[]{:S(2)}) async-start(), calls=%async_computation.3 | async-start | bytes 1179648 | tf_op jit(solution)/shard_map/all_gather | solution.py:52
  8.6 11.6 %collective-permute-start = (bf16[2,256]{1,0:T(2,128)(2,1)S(1)}, bf16[2,256]{1,0:T(2,128)(2,1)S(1)}, u32[]{:S(2)}, u32[]{:S(2)}) collective-permute-start(bf16[2,256]{1,0:T(2,128)(2,1)S(1)} %slice.125), channel_id=1, source_target_pairs={{0,32},{32,64},{64,96},{96,128},{128,160},{160,192},{192,224},{1,3... | collective-permute-start | bytes 3080 | tf_op jit(solution)/shard_map/ppermute | solution.py:11
  13.1 7.1 %collective-permute-start.1 = (bf16[2,256]{1,0:T(2,128)(2,1)S(1)}, bf16[2,256]{1,0:T(2,128)(2,1)S(1)}, u32[]{:S(2)}, u32[]{:S(2)}) collective-permute-start(bf16[2,256]{1,0:T(2,128)(2,1)S(1)} %slice.131), channel_id=1, source_target_pairs={{0,32},{32,64},{64,96},{96,128},{128,160},{160,192},{192,224},{1,3... | collective-permute-start | bytes 3080 | tf_op jit(solution)/shard_map/ppermute | solution.py:11
  21.5 40.3 %all-to-all-start = ((bf16[8,256,256]{2,1,0:T(8,128)(2,1)}), bf16[8,256,256]{2,1,0:T(8,128)(2,1)S(1)}, u32[]{:S(2)}, u32[]{:S(2)}) async-start(bf16[8,256,256]{2,1,0:T(8,128)(2,1)} %stack.44), calls=%async_computation | async-start | bytes 2097152 | tf_op jit(solution)/shard_map/all_to_all | solution.py:60
  28.6 72.7 %all-gather.6.cloned.1.call-start = ((), (), s32[]{:S(2)}) async-start(), calls=%async_computation.4 | async-start | bytes 1179648 | tf_op jit(solution)/shard_map/all_gather | solution.py:53
  29.3 302.2 %reduce-scatter.3.cloned.1.call-start = ((), (), s32[]{:S(2)}) async-start(), calls=%async_computation.5 | async-start | bytes 8650752 | tf_op jit(solution)/shard_map/reduce_scatter | solution.py:82
  29.4 26.8 %collective-permute-start.2 = (bf16[2,256]{1,0:T(2,128)(2,1)S(1)}, bf16[2,256]{1,0:T(2,128)(2,1)S(1)}, u32[]{:S(2)}, u32[]{:S(2)}) collective-permute-start(bf16[2,256]{1,0:T(2,128)(2,1)S(1)} %slice.137), channel_id=1, source_target_pairs={{0,32},{32,64},{64,96},{96,128},{128,160},{160,192},{192,224},{1,3... | collective-permute-start | bytes 3080 | tf_op jit(solution)/shard_map/ppermute | solution.py:11
  101.5 15.7 %copy-start = (f32[256,256]{1,0:T(8,128)S(1)}, f32[256,256]{1,0:T(8,128)}, u32[]{:S(2)}) copy-start(f32[256,256]{1,0:T(8,128)} %convert_element_type.60) | copy-start | bytes 786436
  101.5 15.7 %copy-start.2 = (f32[2,256]{1,0:T(2,128)S(1)}, f32[2,256]{1,0:T(2,128)}, u32[]{:S(2)}) copy-start(f32[2,256]{1,0:T(2,128)} %convert_element_type.61) | copy-start | bytes 6148
  101.5 15.7 %copy-start.3 = (f32[1,1,256]{2,1,0:T(1,128)S(1)}, f32[1,1,256]{2,1,0:T(1,128)}, u32[]{:S(2)}) copy-start(f32[1,1,256]{2,1,0:T(1,128)} %get-tuple-element.237) | copy-start | bytes 3076
  101.5 15.7 %copy-start.4 = (f32[1,1,256]{2,1,0:T(1,128)S(1)}, f32[1,1,256]{2,1,0:T(1,128)}, u32[]{:S(2)}) copy-start(f32[1,1,256]{2,1,0:T(1,128)} %get-tuple-element.244) | copy-start | bytes 3076
  101.5 15.7 %copy-start.5 = (f32[1,1,256]{2,1,0:T(1,128)S(1)}, f32[1,1,256]{2,1,0:T(1,128)}, u32[]{:S(2)}) copy-start(f32[1,1,256]{2,1,0:T(1,128)} %get-tuple-element.245) | copy-start | bytes 3076
  125.2 272.4 %all-gather.8.cloned.1.call-start = ((), (), s32[]{:S(2)}) async-start(), calls=%async_computation.6 | async-start | bytes 8650752 | tf_op jit(solution)/shard_map/all_gather | solution.py:100
  334.3 236.5 %reduce-scatter.5.cloned.1.call-start = ((), (), s32[]{:S(2)}) async-start(), calls=%async_computation.7 | async-start | bytes 2359296 | tf_op jit(solution)/shard_map/reduce_scatter | solution.py:117
Sparse Core Ops, SparseCore 0:
  9.8 48.7 all-gather.3
  60.3 40.9 all-gather.5
  125.3 206.1 reduce-scatter.2
  334.4 63.1 all-gather.7
  422.0 148.7 reduce-scatter.4
